TPU v7x, 128 devices: a whole 4x4x4 slice. The times are simulated.
128 devices in a mesh: phi: 8 (over x, core), eta: 16 (over z, y).
Axes of the slice: x: 4, y: 4, z: 4, core: 2. Of those that a mesh axis runs over, the one named last changes fastest.
Arguments:
- query: bfloat16 [192, 65536], P(None, ('phi', 'eta')), may hold values from -64 to 64
- key_rows: bfloat16 [192, 65536], P(None, ('phi', 'eta')), may hold values from -6 to 6
- value: bfloat16 [192, 65536], P(None, ('phi', 'eta')), may hold values from -6 to 6
- out_grad: bfloat16 [192, 65536], P(None, ('phi', 'eta')), may hold values from -6 to 6
- members: int32 [3, 512, 128], P(None, ('phi', 'eta')), may hold values from 0 to 65535, as said below
Outputs:
- query_grad: bfloat16 [192, 65536], P(None, ('phi', 'eta'))
- key_grad: bfloat16 [192, 65536], P(None, ('phi', 'eta'))
- value_grad: bfloat16 [192, 65536], P(None, ('phi', 'eta'))
Inputs may be any that keep to these rules, and one draw needn't show every extreme that they name: `members`: bucket i of every table is owned by device i // 4 in the order phi+eta, and point id j lies on device j // 512. In each table every point id appears exactly once. In one table a device's buckets hold at most 5 points of any one source device, and exactly 5 for some pairs of devices.
All inputs are finite; a program needn't handle non-finite values.
Results may differ from a plain program's by a relative error of at most 0.0097.
Values may be sent and summed in bfloat16 or wider, within the bound.
A program may use at most 64 MiB of HBM per device.

v0:
```python
import functools

import jax
import jax.numpy as jnp
from jax import lax
from jax.experimental import pallas as pl
from jax.experimental.pallas import tpu as pltpu
from jax.sharding import PartitionSpec as P

HEADS = 8
HEAD_DIM = 24
TABLES = 3
BUCKET = 128
BUCKETS = 12
POINTS = 512
OWNERS = 128
CAP = 5
SLOT = 16
ROWS = OWNERS * SLOT
GROUPS = 2
GH = HEADS // GROUPS
GF = GH * HEAD_DIM
WIDE = 4 * GF
BACK = (256, 384)
CHUNK = 256
STEP_MUL = 37
STEP_INV = 45
MESH = pl.DeviceIdType.MESH
F32 = jnp.float32
BF16 = jnp.bfloat16


def dot(a, b):
    return jnp.dot(a, b, preferred_element_type=F32)


def iota(shape, dim):
    return lax.broadcasted_iota(jnp.int32, shape, dim)


def place():
    phi, eta = lax.axis_index("phi"), lax.axis_index("eta")
    return phi // 2, phi % 2, eta // 4, eta % 4


def peer(step, sign):
    x, core, z, y = place()
    shift = (step * STEP_MUL) % OWNERS
    px = (x + sign * (shift // 32) + 4) % 4
    pc = (core + (shift // 16) % 2) % 2
    pz = (z + sign * ((shift // 4) % 4) + 4) % 4
    py = (y + sign * (shift % 4) + 4) % 4
    return (px * 2 + pc, pz * 4 + py)


def onehot(mask):
    return jnp.where(mask, 1.0, 0.0).astype(BF16)


def kernel(
    query_ref, key_ref, value_ref, grad_ref, members_ref,
    query_out, key_out, value_out,
    columns, wanted, requests, points0, points1, pick, pick_t, gather, gather_t,
    out0, out1, in0, in1, tiles, grads0, grads1, back0, back1, home0, home1,
    send_sem, recv_sem,
):
    points_in, outs, ins = (points0, points1), (out0, out1), (in0, in1)
    grads, backs, homes = (grads0, grads1), (back0, back1), (home0, home1)

    def copy(src, dst, step, sign, number):
        return pltpu.make_async_remote_copy(
            src_ref=src, dst_ref=dst, send_sem=send_sem.at[number], recv_sem=recv_sem.at[number],
            device_id=peer(step, sign), device_id_type=MESH,
        )

    def wait_all(ref, sem):
        pltpu.make_async_copy(ref, ref, sem).wait()

    barrier = pltpu.get_barrier_semaphore()

    @pl.loop(1, OWNERS)
    def _(step):
        pl.semaphore_signal(barrier, inc=1, device_id=peer(step, 1), device_id_type=MESH)

    x, core, z, y = place()
    ids = jnp.concatenate([members_ref[t] for t in range(TABLES)] + [jnp.zeros((4, 128), jnp.int32)], axis=0)
    source, local = ids >> 9, ids & 511
    shift = (
        (((x - (source >> 5)) & 3) << 5)
        | (((core - (source >> 4)) & 1) << 4)
        | (((z - (source >> 2)) & 3) << 2)
        | ((y - source) & 3)
    )
    step_of = (shift * STEP_INV) & (OWNERS - 1)
    both = (step_of * 1024 + local).astype(F32)
    columns[...] = jnp.transpose(jnp.concatenate([both, jnp.zeros((112, 128), F32)], axis=0))
    lane = iota((128, 128), 1)
    sub = iota((128, 128), 0)
    below = onehot(lane < sub)
    asked = jnp.zeros((128, 128), F32)
    codes = jnp.zeros((128, 128), F32)
    for t in range(TABLES):
        seen = jnp.zeros((1, 128), F32)
        for b in range(4):
            n = 4 * t + b
            column = columns[:, n : n + 1].astype(jnp.int32)
            step_col, ask = column >> 10, (column & 1023) + 1
            mine = lane == step_col
            mine_f = jnp.where(mine, 1.0, 0.0)
            earlier = dot(below, mine_f.astype(BF16)) + seen
            rank = jnp.sum(jnp.where(mine, earlier, 0.0), axis=1, keepdims=True).astype(jnp.int32)
            seen = seen + jnp.sum(mine_f, axis=0, keepdims=True)
            slot = CAP * t + rank
            asks = jnp.where(lane == slot, ask >> 4, 0) + jnp.where(lane == slot + SLOT, ask & 15, 0)
            mine_t = onehot(sub == step_of[n : n + 1, :])
            asked = asked + dot(mine_t, asks.astype(F32).astype(BF16))
            codes = jnp.where(lane == n, (SLOT * step_col + slot).astype(F32), codes)
    wanted[...] = asked
    columns[...] = codes
    codes_t = jnp.transpose(codes).astype(jnp.int32)

    pl.semaphore_wait(barrier, OWNERS - 1)

    @pl.loop(1, OWNERS)
    def _(step):
        copy(wanted.at[pl.ds(step, 1)], requests.at[pl.ds(step, 1)], step, -1, 0).start()

    requests[pl.ds(0, 1), :] = asked[0:1, :]
    for g in range(GROUPS):
        rows = pl.ds(g * GF, GF)
        stacked = jnp.concatenate([r[rows, :] for r in (query_ref, key_ref, value_ref, grad_ref)], axis=0)
        points_in[g][...] = jnp.transpose(stacked)
    wait_all(requests.at[pl.ds(1, OWNERS - 1)], recv_sem.at[0])

    asked_low = requests[...].astype(BF16)
    chunk_row = iota((CHUNK, 128), 0)
    chunk_lane = iota((CHUNK, 128), 1)
    weight = jnp.where(chunk_lane == chunk_row % SLOT, 16.0, 0.0) + jnp.where(chunk_lane == chunk_row % SLOT + SLOT, 1.0, 0.0)
    ones = jnp.ones((128, POINTS), BF16)
    number = (iota((CHUNK, POINTS), 1) + 1).astype(F32)

    @pl.loop(0, ROWS // CHUNK)
    def _(k):
        rows = pl.ds(pl.multiple_of(k * CHUNK, CHUNK), CHUNK)
        spread = onehot(chunk_lane == chunk_row // SLOT + k * (CHUNK // SLOT))
        asks = dot(spread, asked_low) * weight
        picked = onehot(dot(asks.astype(BF16), ones) == number)
        pick[rows, :] = picked
        for g in range(GROUPS):
            outs[g][rows, :] = dot(picked, points_in[g][...]).astype(BF16)

    for g in range(GROUPS):

        @pl.loop(1, OWNERS)
        def _(step, g=g):
            rows = pl.ds(pl.multiple_of(step * SLOT, SLOT), SLOT)
            copy(outs[g].at[rows], ins[g].at[rows], step, 1, 1 + g).start()

        ins[g][pl.ds(0, SLOT), :] = outs[g][pl.ds(0, SLOT), :]

    @pl.loop(0, ROWS // CHUNK)
    def _(k):
        rows = pl.ds(pl.multiple_of(k * CHUNK, CHUNK), CHUNK)
        pick_t[:, rows] = jnp.transpose(pick[rows, :])

    for n in range(BUCKETS):
        span = pl.ds(n * BUCKET, BUCKET)
        code = columns[:, n : n + 1].astype(jnp.int32)
        gather[span, :] = onehot(iota((BUCKET, ROWS), 1) == code)
        gather_t[:, span] = onehot(iota((ROWS, BUCKET), 0) == codes_t[n : n + 1, :])

    scale = HEAD_DIM**-0.5
    log2e = 1.4426950408889634
    feature = iota((BUCKET, GF), 1) // HEAD_DIM

    def attend(g, n):
        span = pl.ds(pl.multiple_of(n * BUCKET, BUCKET), BUCKET)
        tile = tiles[span, :]
        full = tile.astype(F32)
        turned = jnp.transpose(full)
        q_low, k_low, v_low, g_low = (tile[:, i * GF : (i + 1) * GF] for i in range(4))
        k_full = full[:, GF : 2 * GF]
        q_t, k_t, v_t, g_t = (turned[i * GF : (i + 1) * GF] for i in range(4))

        def spread_t(part):
            row = iota((GF, BUCKET), 0) // HEAD_DIM
            return jnp.concatenate([jnp.where(row == h, part, 0.0) for h in range(GH)], axis=1).astype(BF16)

        def spread(part):
            return jnp.concatenate([jnp.where(feature == h, part, jnp.zeros_like(part)) for h in range(GH)], axis=0)

        squares = k_full * k_full
        dots = dot(k_low, spread_t(q_t))
        logits = jnp.concatenate(
            [
                dots[:, h * BUCKET : (h + 1) * BUCKET]
                - 0.5 * jnp.sum(jnp.where(feature == h, squares, 0.0), axis=1, keepdims=True)
                for h in range(GH)
            ],
            axis=1,
        )
        top = jnp.max(logits, axis=0, keepdims=True)
        expons = jnp.exp2((logits - top) * (scale * log2e))
        probs = expons * (1.0 / jnp.sum(expons, axis=0, keepdims=True))
        probs_low = probs.astype(BF16)
        dprob = dot(v_low, spread_t(g_t))

        def paired(left, right):
            left = left.astype(BF16)
            parts = []
            for u in range(GH // 2):
                both = dot(left[2 * HEAD_DIM * u : 2 * HEAD_DIM * (u + 1)], right[:, 2 * BUCKET * u : 2 * BUCKET * (u + 1)])
                parts += [both[:HEAD_DIM, :BUCKET], both[HEAD_DIM:, BUCKET:]]
            return parts

        delta = jnp.concatenate(
            [
                jnp.sum(part * g_t[h * HEAD_DIM : (h + 1) * HEAD_DIM], axis=0, keepdims=True)
                for h, part in enumerate(paired(v_t, probs_low))
            ],
            axis=1,
        )
        dscore = scale * probs * (dprob - delta)
        dscore_low = dscore.astype(BF16)
        query_part = jnp.transpose(jnp.concatenate(paired(k_t, dscore_low), axis=0)).astype(BF16)
        sums = jnp.zeros((BUCKET, GF), F32)
        for h in range(GH):
            total = jnp.sum(dscore[:, h * BUCKET : (h + 1) * BUCKET], axis=1, keepdims=True)
            sums = jnp.where(feature == h, total, sums)
        key_part = (dot(dscore_low, spread(q_low)) - sums * k_full).astype(BF16)
        value_part = dot(probs_low, spread(g_low)).astype(BF16)
        if g == 0:
            grads0[span, :] = jnp.concatenate([query_part, key_part, value_part[:, :64]], axis=1)
            grads1[span, 288:320] = value_part[:, 64:]
        else:
            grads1[span, 0:288] = jnp.concatenate([query_part, key_part, value_part], axis=1)

    grads1[:, 256:384] = jnp.zeros((BUCKETS * BUCKET, 128), BF16)
    for g in range(GROUPS):
        wait_all(ins[g].at[pl.ds(SLOT, ROWS - SLOT)], recv_sem.at[1 + g])

        @pl.loop(0, TABLES)
        def _(t, g=g):
            rows = pl.ds(pl.multiple_of(t * POINTS, POINTS), POINTS)
            tiles[rows, :] = dot(gather[rows, :], ins[g][...]).astype(BF16)

        @pl.loop(0, BUCKETS)
        def _(n, g=g):
            attend(g, n)

        @pl.loop(0, ROWS // CHUNK)
        def _(k, g=g):
            rows = pl.ds(pl.multiple_of(k * CHUNK, CHUNK), CHUNK)
            backs[g][rows, :] = dot(gather_t[rows, :], grads[g][...]).astype(BF16)

        @pl.loop(1, OWNERS)
        def _(step, g=g):
            rows = pl.ds(pl.multiple_of(step * SLOT, SLOT), SLOT)
            copy(backs[g].at[rows], homes[g].at[rows], step, -1, 3 + g).start()

        homes[g][pl.ds(0, SLOT), :] = backs[g][pl.ds(0, SLOT), :]

    for g in range(GROUPS):
        wait_all(homes[g].at[pl.ds(SLOT, ROWS - SLOT)], recv_sem.at[3 + g])
        result = jnp.transpose(dot(pick_t[...], homes[g][...])).astype(BF16)
        mine = pl.ds(g * GF, GF)
        query_out[mine, :] = result[0:GF]
        key_out[mine, :] = result[GF : 2 * GF]
        if g == 0:
            value_out[pl.ds(0, 64), :] = result[192:256]
        else:
            value_out[mine, :] = result[192:288]
            value_out[pl.ds(64, 32), :] = result[288:320]

    wait_all(wanted.at[pl.ds(1, OWNERS - 1)], send_sem.at[0])
    for g in range(GROUPS):
        wait_all(outs[g].at[pl.ds(SLOT, ROWS - SLOT)], send_sem.at[1 + g])
        wait_all(backs[g].at[pl.ds(SLOT, ROWS - SLOT)], send_sem.at[3 + g])


def on_device(query, key_rows, value, out_grad, members):
    shape = jax.ShapeDtypeStruct(query.shape, BF16)
    vmem = pl.BlockSpec(memory_space=pltpu.VMEM)
    return pl.pallas_call(
        kernel,
        name="hept_backward",
        out_shape=(shape, shape, shape),
        in_specs=[vmem] * 5,
        out_specs=(vmem,) * 3,
        scratch_shapes=[
            pltpu.VMEM((128, 128), F32),
            pltpu.VMEM((128, 128), F32),
            pltpu.VMEM((128, 128), F32),
            pltpu.VMEM((POINTS, WIDE), BF16),
            pltpu.VMEM((POINTS, WIDE), BF16),
            pltpu.VMEM((ROWS, POINTS), BF16),
            pltpu.VMEM((POINTS, ROWS), BF16),
            pltpu.VMEM((BUCKETS * BUCKET, ROWS), BF16),
            pltpu.VMEM((ROWS, BUCKETS * BUCKET), BF16),
            pltpu.VMEM((ROWS, WIDE), BF16),
            pltpu.VMEM((ROWS, WIDE), BF16),
            pltpu.VMEM((ROWS, WIDE), BF16),
            pltpu.VMEM((ROWS, WIDE), BF16),
            pltpu.VMEM((BUCKETS * BUCKET, WIDE), BF16),
            pltpu.VMEM((BUCKETS * BUCKET, BACK[0]), BF16),
            pltpu.VMEM((BUCKETS * BUCKET, BACK[1]), BF16),
            pltpu.VMEM((ROWS, BACK[0]), BF16),
            pltpu.VMEM((ROWS, BACK[1]), BF16),
            pltpu.VMEM((ROWS, BACK[0]), BF16),
            pltpu.VMEM((ROWS, BACK[1]), BF16),
            pltpu.SemaphoreType.DMA((5,)),
            pltpu.SemaphoreType.DMA((5,)),
        ],
        compiler_params=pltpu.CompilerParams(
            collective_id=0, has_side_effects=True, vmem_limit_bytes=56 * 1024 * 1024
        ),
    )(query, key_rows, value, out_grad, members)


def solution(mesh):
    in_specs = (
        P(None, ("phi", "eta")),
        P(None, ("phi", "eta")),
        P(None, ("phi", "eta")),
        P(None, ("phi", "eta")),
        P(None, ("phi", "eta"), None),
    )
    out_specs = (P(None, ("phi", "eta")), P(None, ("phi", "eta")), P(None, ("phi", "eta")))
    return jax.shard_map(
        on_device, mesh=mesh, in_specs=in_specs, out_specs=out_specs, check_vma=False
    )
```

profile of v0, /device:TPU:1, one launch (start us, length us, event | category | flops | bytes accessed | tf_op | source)
XLA Modules:
  0.0 125.1 jit_solution(12820977105503871555)
XLA Ops:
  0.6 121.1 %hept_backward.1 = (bf16[192,512]{1,0:T(8,128)(2,1)}, bf16[192,512]{1,0:T(8,128)(2,1)}, bf16[192,512]{1,0:T(8,128)(2,1)}) custom-call(bf16[192,512]{1,0:T(8,128)(2,1)} %query_ref.1, bf16[192,512]{1,0:T(8,128)(2,1)} %key_ref.1, bf16[192,512]{1,0:T(8,128)(2,1)} %value_ref.1, bf16[192,512]{1,0:T(8,128)(2,1)} %grad_ref.1, s32[3,4,128]{2,1,0:T(4,128)} %members_ref.1), custom_call_target="tpu_custom_call" | custom-call | tf_op jit(solution)/shard_map/hept_backward/pallas_call | solution.py:284
  121.7 0.0 copy-start.1
  121.7 1.7 %copy.11 = bf16[192,512]{1,0:T(8,128)(2,1)} copy(bf16[192,512]{1,0:T(8,128)(2,1)} %get-tuple-element.6) | data formatting | bytes 393216
  123.4 0.0 copy-done.1
  123.4 0.0 copy-start
  123.4 0.7 copy.12
  124.1 0.3 copy-done
  124.4 0.7 copy.13
Async XLA Ops:
  121.7 1.7 %copy-start.1 = (bf16[192,512]{1,0:T(8,128)(2,1)S(1)}, bf16[192,512]{1,0:T(8,128)(2,1)}, u32[]{:S(2)}) copy-start(bf16[192,512]{1,0:T(8,128)(2,1)} %get-tuple-element.7) | copy-start | bytes 589828
  123.4 1.0 copy-start
where the time goes:
time: 125 us
  Pallas kernels  121 us (97%)
  local copies, waits for them, and re-layouts  3.33 us (3%)
    pallas_call x1, Pallas kernels, on_device(): pl.pallas_call(kernel, name='hept_backward', out_shape=(shape, shape, sha...  121 us
    unnamed x7, local copies, waits for them, and re-layouts  3.33 us

commit v1 on v0

v1 whole, which is shorter than its diff:
```python
import functools

import jax
import jax.numpy as jnp
from jax import lax
from jax.experimental import pallas as pl
from jax.experimental.pallas import tpu as pltpu
from jax.sharding import PartitionSpec as P

HEADS = 8
HEAD_DIM = 24
TABLES = 3
BUCKET = 128
BUCKETS = 12
POINTS = 512
OWNERS = 128
CAP = 5
SLOT = 16
ROWS = OWNERS * SLOT
TROWS = OWNERS * CAP
GROUPS = 2
GH = HEADS // GROUPS
GF = GH * HEAD_DIM
WIDE = 4 * GF
BACK = (256, 384)
CHUNK = 256
CHUNKS = ROWS // CHUNK
PER = CHUNK // SLOT
TCHUNK = PER * CAP
TOGETHER = 2
STEP_MUL = 37
STEP_INV = 45
MESH = pl.DeviceIdType.MESH
F32 = jnp.float32
BF16 = jnp.bfloat16


def dot(a, b):
    return jnp.dot(a, b, preferred_element_type=F32)


def iota(shape, dim):
    return lax.broadcasted_iota(jnp.int32, shape, dim)


def place():
    phi, eta = lax.axis_index("phi"), lax.axis_index("eta")
    return phi // 2, phi % 2, eta // 4, eta % 4


def torus():
    x, core, z, y = place()
    xs = [((x + a) % 4) * 2 for a in range(4)]
    cores = [core, 1 - core]
    zs = [((z + a) % 4) * 4 for a in range(4)]
    ys = [(y + a) % 4 for a in range(4)]

    def peer(step, sign):
        shift = (step * STEP_MUL) % OWNERS
        a, c, d = (sign * (shift // n) % 4 for n in (32, 4, 1))
        return (xs[a] + cores[shift // 16 % 2], zs[c] + ys[d])

    return peer


def onehot(mask):
    return jnp.where(mask, 1.0, 0.0).astype(BF16)


def kernel(
    query_any, key_any, value_any, grad_any, members_any,
    query_out, key_out, value_out,
    query_ref, key_ref, value_ref, grad_ref, members_ref,
    columns, wanted, requests, points0, points1, pick, pick_t, gather, gather_t,
    out0, out1, in0, in1, rows_of, tiles, grads0, grads1, slots0, slots1, back0, back1, home0, home1,
    load_sem, send_sem, recv_sem,
):
    points_in, outs, ins = (points0, points1), (out0, out1), (in0, in1)
    grads, slots, backs, homes = (grads0, grads1), (slots0, slots1), (back0, back1), (home0, home1)
    peer = torus()

    def copy(src, dst, step, sign, sent, received):
        return pltpu.make_async_remote_copy(
            src_ref=src, dst_ref=dst, send_sem=send_sem.at[sent], recv_sem=recv_sem.at[received],
            device_id=peer(step, sign), device_id_type=MESH,
        )

    def wait_all(ref, sem):
        pltpu.make_async_copy(ref, ref, sem).wait()

    barrier = pltpu.get_barrier_semaphore()
    loads = [
        pltpu.make_async_copy(src, dst, load_sem.at[i])
        for i, (src, dst) in enumerate(
            [
                (members_any, members_ref),
                (query_any, query_ref),
                (key_any, key_ref),
                (value_any, value_ref),
                (grad_any, grad_ref),
            ]
        )
    ]
    for load in loads:
        load.start()
    for step in range(1, OWNERS):
        pl.semaphore_signal(barrier, inc=1, device_id=peer(step, 1), device_id_type=MESH)
    loads[0].wait()

    x, core, z, y = place()
    ids = jnp.concatenate([members_ref[t] for t in range(TABLES)] + [jnp.zeros((4, 128), jnp.int32)], axis=0)
    source, local = ids >> 9, ids & 511
    shift = (
        (((x - (source >> 5)) & 3) << 5)
        | (((core - (source >> 4)) & 1) << 4)
        | (((z - (source >> 2)) & 3) << 2)
        | ((y - source) & 3)
    )
    step_of = (shift * STEP_INV) & (OWNERS - 1)
    both = (step_of * 1024 + local).astype(F32)
    columns[...] = jnp.transpose(jnp.concatenate([both, jnp.zeros((112, 128), F32)], axis=0))
    lane = iota((128, 128), 1)
    sub = iota((128, 128), 0)
    below = onehot(lane < sub)
    asked = jnp.zeros((128, 128), F32)
    codes = jnp.zeros((128, 128), F32)
    for t in range(TABLES):
        seen = jnp.zeros((1, 128), F32)
        for b in range(4):
            n = 4 * t + b
            column = columns[:, n : n + 1].astype(jnp.int32)
            step_col, ask = column >> 10, (column & 1023) + 1
            mine = lane == step_col
            mine_f = jnp.where(mine, 1.0, 0.0)
            earlier = dot(below, mine_f.astype(BF16)) + seen
            rank = jnp.sum(jnp.where(mine, earlier, 0.0), axis=1, keepdims=True).astype(jnp.int32)
            seen = seen + jnp.sum(mine_f, axis=0, keepdims=True)
            slot = CAP * t + rank
            asks = jnp.where(lane == slot, ask >> 4, 0) + jnp.where(lane == slot + SLOT, ask & 15, 0)
            mine_t = onehot(sub == step_of[n : n + 1, :])
            asked = asked + dot(mine_t, asks.astype(F32).astype(BF16))
            codes = jnp.where(lane == n, (CAP * step_col + rank).astype(F32), codes)
    wanted[...] = asked
    columns[...] = codes

    pl.semaphore_wait(barrier, OWNERS - 1)
    for step in range(1, OWNERS):
        row = pl.ds(step, 1)
        copy(wanted.at[row], requests.at[row], step, -1, 0, step // PER).start()
    requests[pl.ds(0, 1), :] = asked[0:1, :]
    for load in loads[1:]:
        load.wait()

    def turn_points(g):
        rows = pl.ds(g * GF, GF)
        stacked = jnp.concatenate([r[rows, :] for r in (query_ref, key_ref, value_ref, grad_ref)], axis=0)
        points_in[g][...] = jnp.transpose(stacked)

    chunk_row = iota((CHUNK, 128), 0)
    chunk_lane = iota((CHUNK, 128), 1)
    weight = jnp.where(chunk_lane == chunk_row % SLOT, 16.0, 0.0) + jnp.where(chunk_lane == chunk_row % SLOT + SLOT, 1.0, 0.0)
    spread = onehot(iota((CHUNK, PER), 1) == iota((CHUNK, PER), 0) // SLOT)
    ones = jnp.ones((128, POINTS), BF16)
    number = (iota((CHUNK, POINTS), 1) + 1).astype(F32)

    def send(src, dst, k, sign, number):
        for step in range(max(1, k * PER), (k + 1) * PER):
            rows = pl.ds(step * SLOT, SLOT)
            copy(src.at[rows], dst.at[rows], step, sign, number, CHUNKS - 1 + number).start()
        if k == 0:
            dst[pl.ds(0, SLOT), :] = src[pl.ds(0, SLOT), :]

    turn_points(0)
    for k in range(CHUNKS):
        rows = pl.ds(k * CHUNK, CHUNK)
        wait_all(requests.at[pl.ds(max(1, k * PER), PER - (k == 0))], recv_sem.at[k])
        asks = dot(spread, requests[pl.ds(k * PER, PER), :].astype(BF16)) * weight
        picked = onehot(dot(asks.astype(BF16), ones) == number)
        pick[rows, :] = picked
        out0[rows, :] = dot(picked, points0[...]).astype(BF16)
        send(out0, in0, k, 1, 1)
    turn_points(1)
    for k in range(CHUNKS):
        rows = pl.ds(k * CHUNK, CHUNK)
        out1[rows, :] = dot(pick[rows, :], points1[...]).astype(BF16)
        send(out1, in1, k, 1, 2)

    @pl.loop(0, CHUNKS)
    def _(k):
        rows = pl.ds(pl.multiple_of(k * CHUNK, CHUNK), CHUNK)
        pick_t[:, rows] = jnp.transpose(pick[rows, :])

    codes_t = jnp.transpose(columns[...]).astype(jnp.int32)
    for n in range(BUCKETS):
        t, b = n // 4, n % 4
        code = columns[:, n : n + 1].astype(jnp.int32)
        gather[pl.ds(n * BUCKET, BUCKET), :] = onehot(iota((BUCKET, TROWS), 1) == code)
        gather_t[t, :, pl.ds(b * BUCKET, BUCKET)] = onehot(iota((TROWS, BUCKET), 0) == codes_t[n : n + 1, :])

    packed_row = iota((TABLES * TCHUNK, CHUNK), 0)
    within = packed_row % TCHUNK
    split = onehot(
        iota((TABLES * TCHUNK, CHUNK), 1) == SLOT * (within // CAP) + CAP * (packed_row // TCHUNK) + within % CAP
    )
    packed_lane = iota((CHUNK, TABLES * TCHUNK), 1)
    within = packed_lane % TCHUNK
    merge = onehot(
        iota((CHUNK, TABLES * TCHUNK), 0) == SLOT * (within // CAP) + CAP * (packed_lane // TCHUNK) + within % CAP
    )

    scale = HEAD_DIM**-0.5
    log2e = 1.4426950408889634
    feature = iota((BUCKET, GF), 1) // HEAD_DIM
    heads = [onehot(feature == h) for h in range(GH)]

    def attend(g, n):
        span = pl.ds(pl.multiple_of(n * BUCKET, BUCKET), BUCKET)
        tile = tiles[span, :]
        full = tile.astype(F32)
        turned = jnp.transpose(full)
        q_low, k_low, v_low, g_low = (tile[:, i * GF : (i + 1) * GF] for i in range(4))
        k_full = full[:, GF : 2 * GF]
        q_t, k_t, v_t, g_t = (turned[i * GF : (i + 1) * GF] for i in range(4))

        def spread_t(part):
            blocks = []
            for h in range(GH):
                pieces = [part[h * HEAD_DIM : (h + 1) * HEAD_DIM]]
                if h > 0:
                    pieces = [jnp.zeros((h * HEAD_DIM, BUCKET), F32)] + pieces
                if h < GH - 1:
                    pieces = pieces + [jnp.zeros(((GH - 1 - h) * HEAD_DIM, BUCKET), F32)]
                blocks.append(jnp.concatenate(pieces, axis=0))
            return jnp.concatenate(blocks, axis=1).astype(BF16)

        def spread_rows(part):
            return jnp.concatenate([part * head for head in heads], axis=0)

        squares = k_full * k_full
        dots = dot(k_low, spread_t(q_t))
        dprob = dot(v_low, spread_t(g_t))
        yield
        logits = jnp.concatenate(
            [
                dots[:, h * BUCKET : (h + 1) * BUCKET]
                - 0.5 * jnp.sum(jnp.where(feature == h, squares, 0.0), axis=1, keepdims=True)
                for h in range(GH)
            ],
            axis=1,
        )
        top = jnp.max(logits, axis=0, keepdims=True)
        expons = jnp.exp2((logits - top) * (scale * log2e))
        probs = expons * (1.0 / jnp.sum(expons, axis=0, keepdims=True))
        probs_low = probs.astype(BF16)
        yield

        def paired(left, right):
            left = left.astype(BF16)
            parts = []
            for u in range(GH // 2):
                both = dot(left[2 * HEAD_DIM * u : 2 * HEAD_DIM * (u + 1)], right[:, 2 * BUCKET * u : 2 * BUCKET * (u + 1)])
                parts += [both[:HEAD_DIM, :BUCKET], both[HEAD_DIM:, BUCKET:]]
            return parts

        delta = jnp.concatenate(
            [
                jnp.sum(part * g_t[h * HEAD_DIM : (h + 1) * HEAD_DIM], axis=0, keepdims=True)
                for h, part in enumerate(paired(v_t, probs_low))
            ],
            axis=1,
        )
        value_part = dot(probs_low, spread_rows(g_low)).astype(BF16)
        yield
        dscore = scale * probs * (dprob - delta)
        dscore_low = dscore.astype(BF16)
        sums = jnp.zeros((BUCKET, GF), F32)
        for h in range(GH):
            total = jnp.sum(dscore[:, h * BUCKET : (h + 1) * BUCKET], axis=1, keepdims=True)
            sums = jnp.where(feature == h, total, sums)
        yield
        query_part = jnp.transpose(jnp.concatenate(paired(k_t, dscore_low), axis=0)).astype(BF16)
        key_part = (dot(dscore_low, spread_rows(q_low)) - sums * k_full).astype(BF16)
        if g == 0:
            grads0[span, :] = jnp.concatenate([query_part, key_part, value_part[:, :64]], axis=1)
            grads1[span, 288:320] = value_part[:, 64:]
        else:
            grads1[span, 0:288] = jnp.concatenate([query_part, key_part, value_part], axis=1)

    grads1[:, 256:384] = jnp.zeros((BUCKETS * BUCKET, 128), BF16)
    for g in range(GROUPS):
        wait_all(ins[g].at[pl.ds(SLOT, ROWS - SLOT)], recv_sem.at[CHUNKS + g])
        for k in range(CHUNKS):
            part = dot(split, ins[g][pl.ds(k * CHUNK, CHUNK), :]).astype(BF16)
            for t in range(TABLES):
                rows_of[t, pl.ds(k * TCHUNK, TCHUNK), :] = part[t * TCHUNK : (t + 1) * TCHUNK]
        for t in range(TABLES):
            rows = pl.ds(t * POINTS, POINTS)
            tiles[rows, :] = dot(gather[rows, :], rows_of[t]).astype(BF16)

        @pl.loop(0, BUCKETS // TOGETHER)
        def _(n, g=g):
            running = [attend(g, n * TOGETHER + i) for i in range(TOGETHER)]
            while running:
                running = [r for r in running if next(r, 0) is None]

        for t in range(TABLES):
            slots[g][t] = dot(gather_t[t], grads[g][pl.ds(t * POINTS, POINTS), :]).astype(BF16)
        for k in range(CHUNKS):
            part = jnp.concatenate([slots[g][t, pl.ds(k * TCHUNK, TCHUNK), :] for t in range(TABLES)], axis=0)
            backs[g][pl.ds(k * CHUNK, CHUNK), :] = dot(merge, part).astype(BF16)
            send(backs[g], homes[g], k, -1, 3 + g)

    for g in range(GROUPS):
        wait_all(homes[g].at[pl.ds(SLOT, ROWS - SLOT)], recv_sem.at[CHUNKS + 2 + g])
        result = jnp.transpose(dot(pick_t[...], homes[g][...])).astype(BF16)
        mine = pl.ds(g * GF, GF)
        query_out[mine, :] = result[0:GF]
        key_out[mine, :] = result[GF : 2 * GF]
        if g == 0:
            value_out[pl.ds(0, 64), :] = result[192:256]
        else:
            value_out[mine, :] = result[192:288]
            value_out[pl.ds(64, 32), :] = result[288:320]

    wait_all(wanted.at[pl.ds(1, OWNERS - 1)], send_sem.at[0])
    for g in range(GROUPS):
        wait_all(outs[g].at[pl.ds(SLOT, ROWS - SLOT)], send_sem.at[1 + g])
        wait_all(backs[g].at[pl.ds(SLOT, ROWS - SLOT)], send_sem.at[3 + g])


def on_device(query, key_rows, value, out_grad, members):
    shape = jax.ShapeDtypeStruct(query.shape, BF16)
    vmem = pl.BlockSpec(memory_space=pltpu.VMEM)
    return pl.pallas_call(
        kernel,
        name="hept_backward",
        out_shape=(shape, shape, shape),
        in_specs=[pl.BlockSpec(memory_space=pl.ANY)] * 5,
        out_specs=(vmem,) * 3,
        scratch_shapes=[
            *[pltpu.VMEM(query.shape, BF16)] * 4,
            pltpu.VMEM(members.shape, jnp.int32),
            *[pltpu.VMEM((128, 128), F32)] * 3,
            *[pltpu.VMEM((POINTS, WIDE), BF16)] * 2,
            pltpu.VMEM((ROWS, POINTS), BF16),
            pltpu.VMEM((POINTS, ROWS), BF16),
            pltpu.VMEM((BUCKETS * BUCKET, TROWS), BF16),
            pltpu.VMEM((TABLES, TROWS, POINTS), BF16),
            *[pltpu.VMEM((ROWS, WIDE), BF16)] * 4,
            pltpu.VMEM((TABLES, TROWS, WIDE), BF16),
            pltpu.VMEM((BUCKETS * BUCKET, WIDE), BF16),
            *[pltpu.VMEM((BUCKETS * BUCKET, width), BF16) for width in BACK],
            *[pltpu.VMEM((TABLES, TROWS, width), BF16) for width in BACK],
            *[pltpu.VMEM((ROWS, width), BF16) for width in BACK],
            *[pltpu.VMEM((ROWS, width), BF16) for width in BACK],
            pltpu.SemaphoreType.DMA((5,)),
            pltpu.SemaphoreType.DMA((5,)),
            pltpu.SemaphoreType.DMA((CHUNKS + 4,)),
        ],
        compiler_params=pltpu.CompilerParams(
            collective_id=0, has_side_effects=True, vmem_limit_bytes=56 * 1024 * 1024
        ),
    )(query, key_rows, value, out_grad, members)


def solution(mesh):
    in_specs = (
        P(None, ("phi", "eta")),
        P(None, ("phi", "eta")),
        P(None, ("phi", "eta")),
        P(None, ("phi", "eta")),
        P(None, ("phi", "eta"), None),
    )
    out_specs = (P(None, ("phi", "eta")), P(None, ("phi", "eta")), P(None, ("phi", "eta")))
    return jax.shard_map(
        on_device, mesh=mesh, in_specs=in_specs, out_specs=out_specs, check_vma=False
    )
```

time: 125 us -> 94.3 us (0.75); the launches traced: 125 us -> 92.9 us
  Pallas kernels: 121 us -> 88.9 us
    pallas_call x1, Pallas kernels: 121 us -> 88.9 us  [on_device(): pl.pallas_call(kernel, name='hept_backward', out_shape=(shape, shape, sha...]
where the time goes in v1:
time: 94.3 us; the launch traced here: 92.9 us
  Pallas kernels  88.9 us (94%)
  local copies, waits for them, and re-layouts  3.33 us (4%)
    pallas_call x1, Pallas kernels, on_device(): pl.pallas_call(kernel, name='hept_backward', out_shape=(shape, shape, sha...  88.9 us
    unnamed x7, local copies, waits for them, and re-layouts  3.33 us

profile of v1, /device:TPU:1, one launch (start us, length us, event | category | flops | bytes accessed | tf_op | source)
XLA Modules:
  0.0 92.9 jit_solution(17472432492320949089)
XLA Ops:
  0.6 88.9 %hept_backward.1 = (bf16[192,512]{1,0:T(8,128)(2,1)}, bf16[192,512]{1,0:T(8,128)(2,1)}, bf16[192,512]{1,0:T(8,128)(2,1)}) custom-call(bf16[192,512]{1,0:T(8,128)(2,1)} %query_any.1, bf16[192,512]{1,0:T(8,128)(2,1)} %key_any.1, bf16[192,512]{1,0:T(8,128)(2,1)} %value_any.1, bf16[192,512]{1,0:T(8,128)(2,1)} %grad_any.1, s32[3,4,128]{2,1,0:T(4,128)} %members_any.1), custom_call_target="tpu_custom_call" | custom-call | tf_op jit(solution)/shard_map/hept_backward/pallas_call | solution.py:334
  89.5 0.0 copy-start.1
  89.6 1.7 %copy.11 = bf16[192,512]{1,0:T(8,128)(2,1)} copy(bf16[192,512]{1,0:T(8,128)(2,1)} %get-tuple-element.6) | data formatting | bytes 393216
  91.2 0.0 copy-done.1
  91.2 0.0 copy-start
  91.2 0.7 copy.12
  91.9 0.3 copy-done
  92.2 0.7 copy.13
Async XLA Ops:
  89.5 1.7 %copy-start.1 = (bf16[192,512]{1,0:T(8,128)(2,1)S(1)}, bf16[192,512]{1,0:T(8,128)(2,1)}, u32[]{:S(2)}) copy-start(bf16[192,512]{1,0:T(8,128)(2,1)} %get-tuple-element.7) | copy-start | bytes 589828
  91.2 1.0 %copy-start = (bf16[192,512]{1,0:T(8,128)(2,1)S(1)}, bf16[192,512]{1,0:T(8,128)(2,1)}, u32[]{:S(2)}) copy-start(bf16[192,512]{1,0:T(8,128)(2,1)} %get-tuple-element.8) | copy-start | bytes 589828

commit v2 on v1

--- a/solution.py
+++ b/solution.py
@@ -22,14 +22,21 @@
 GH = HEADS // GROUPS
 GF = GH * HEAD_DIM
 WIDE = 4 * GF
+FEAT = HEADS * HEAD_DIM
 BACK = (256, 384)
 CHUNK = 256
 CHUNKS = ROWS // CHUNK
 PER = CHUNK // SLOT
 TCHUNK = PER * CAP
 TOGETHER = 2
-STEP_MUL = 37
-STEP_INV = 45
+PARTS = 4
+
+
+def hops(shift):
+    return sum((0, 1, 2, 1)[shift // n % 4] for n in (32, 4, 1))
+
+
+ORDER = [0] + sorted(((j * 37) % OWNERS for j in range(1, OWNERS)), key=hops)
 MESH = pl.DeviceIdType.MESH
 F32 = jnp.float32
 BF16 = jnp.bfloat16
@@ -56,7 +63,7 @@
     ys = [(y + a) % 4 for a in range(4)]
 
     def peer(step, sign):
-        shift = (step * STEP_MUL) % OWNERS
+        shift = ORDER[step]
         a, c, d = (sign * (shift // n) % 4 for n in (32, 4, 1))
         return (xs[a] + cores[shift // 16 % 2], zs[c] + ys[d])
 
@@ -69,7 +76,7 @@
 
 def kernel(
     query_any, key_any, value_any, grad_any, members_any,
-    query_out, key_out, value_out,
+    result_ref,
     query_ref, key_ref, value_ref, grad_ref, members_ref,
     columns, wanted, requests, points0, points1, pick, pick_t, gather, gather_t,
     out0, out1, in0, in1, rows_of, tiles, grads0, grads1, slots0, slots1, back0, back1, home0, home1,
@@ -116,7 +123,9 @@
         | (((z - (source >> 2)) & 3) << 2)
         | ((y - source) & 3)
     )
-    step_of = (shift * STEP_INV) & (OWNERS - 1)
+    step_of = jnp.zeros_like(shift)
+    for step in range(1, OWNERS):
+        step_of = jnp.where(shift == ORDER[step], step, step_of)
     both = (step_of * 1024 + local).astype(F32)
     columns[...] = jnp.transpose(jnp.concatenate([both, jnp.zeros((112, 128), F32)], axis=0))
     lane = iota((128, 128), 1)
@@ -144,6 +153,7 @@
     columns[...] = codes
 
     pl.semaphore_wait(barrier, OWNERS - 1)
+
     for step in range(1, OWNERS):
         row = pl.ds(step, 1)
         copy(wanted.at[row], requests.at[row], step, -1, 0, step // PER).start()
@@ -163,10 +173,10 @@
     ones = jnp.ones((128, POINTS), BF16)
     number = (iota((CHUNK, POINTS), 1) + 1).astype(F32)
 
-    def send(src, dst, k, sign, number):
+    def send(src, dst, k, sign, number, received):
         for step in range(max(1, k * PER), (k + 1) * PER):
             rows = pl.ds(step * SLOT, SLOT)
-            copy(src.at[rows], dst.at[rows], step, sign, number, CHUNKS - 1 + number).start()
+            copy(src.at[rows], dst.at[rows], step, sign, number, received).start()
         if k == 0:
             dst[pl.ds(0, SLOT), :] = src[pl.ds(0, SLOT), :]
 
@@ -178,12 +188,12 @@
         picked = onehot(dot(asks.astype(BF16), ones) == number)
         pick[rows, :] = picked
         out0[rows, :] = dot(picked, points0[...]).astype(BF16)
-        send(out0, in0, k, 1, 1)
+        send(out0, in0, k, 1, 1, CHUNKS)
     turn_points(1)
     for k in range(CHUNKS):
         rows = pl.ds(k * CHUNK, CHUNK)
         out1[rows, :] = dot(pick[rows, :], points1[...]).astype(BF16)
-        send(out1, in1, k, 1, 2)
+        send(out1, in1, k, 1, 2, CHUNKS + 1)
 
     @pl.loop(0, CHUNKS)
     def _(k):
@@ -212,6 +222,7 @@
     log2e = 1.4426950408889634
     feature = iota((BUCKET, GF), 1) // HEAD_DIM
     heads = [onehot(feature == h) for h in range(GH)]
+    term_heads = onehot(iota((24, GH * BUCKET), 0) % 8 == iota((24, GH * BUCKET), 1) // BUCKET)
 
     def attend(g, n):
         span = pl.ds(pl.multiple_of(n * BUCKET, BUCKET), BUCKET)
@@ -236,18 +247,22 @@
         def spread_rows(part):
             return jnp.concatenate([part * head for head in heads], axis=0)
 
-        squares = k_full * k_full
-        dots = dot(k_low, spread_t(q_t))
+        norms = jnp.concatenate(
+            [
+                -0.5 * jnp.sum(k_t[h * HEAD_DIM : (h + 1) * HEAD_DIM] ** 2, axis=0, keepdims=True)
+                for h in range(GH)
+            ]
+            + [jnp.zeros((8 - GH, BUCKET), F32)],
+            axis=0,
+        )
+        terms = []
+        for _ in range(3):
+            terms.append(norms.astype(BF16).astype(F32))
+            norms = norms - terms[-1]
+        terms = jnp.transpose(jnp.concatenate(terms, axis=0)).astype(BF16)
+        logits = dot(jnp.concatenate([k_low, terms], axis=1), jnp.concatenate([spread_t(q_t), term_heads], axis=0))
         dprob = dot(v_low, spread_t(g_t))
         yield
-        logits = jnp.concatenate(
-            [
-                dots[:, h * BUCKET : (h + 1) * BUCKET]
-                - 0.5 * jnp.sum(jnp.where(feature == h, squares, 0.0), axis=1, keepdims=True)
-                for h in range(GH)
-            ],
-            axis=1,
-        )
         top = jnp.max(logits, axis=0, keepdims=True)
         expons = jnp.exp2((logits - top) * (scale * log2e))
         probs = expons * (1.0 / jnp.sum(expons, axis=0, keepdims=True))
@@ -308,19 +323,22 @@
         for k in range(CHUNKS):
             part = jnp.concatenate([slots[g][t, pl.ds(k * TCHUNK, TCHUNK), :] for t in range(TABLES)], axis=0)
             backs[g][pl.ds(k * CHUNK, CHUNK), :] = dot(merge, part).astype(BF16)
-            send(backs[g], homes[g], k, -1, 3 + g)
+            send(backs[g], homes[g], k, -1, 3 + g, CHUNKS + GROUPS + g * PARTS + k // (CHUNKS // PARTS))
 
     for g in range(GROUPS):
-        wait_all(homes[g].at[pl.ds(SLOT, ROWS - SLOT)], recv_sem.at[CHUNKS + 2 + g])
-        result = jnp.transpose(dot(pick_t[...], homes[g][...])).astype(BF16)
-        mine = pl.ds(g * GF, GF)
-        query_out[mine, :] = result[0:GF]
-        key_out[mine, :] = result[GF : 2 * GF]
+        total = jnp.zeros((POINTS, BACK[g]), F32)
+        for p in range(PARTS):
+            part = ROWS // PARTS
+            wait_all(homes[g].at[pl.ds(max(SLOT, p * part), part - SLOT * (p == 0))], recv_sem.at[CHUNKS + GROUPS + g * PARTS + p])
+            total = total + dot(pick_t[:, p * part : (p + 1) * part], homes[g][pl.ds(p * part, part), :])
+        result = jnp.transpose(total).astype(BF16)
+        for i in range(2):
+            result_ref[pl.ds(i * FEAT + g * GF, GF), :] = result[i * GF : (i + 1) * GF]
         if g == 0:
-            value_out[pl.ds(0, 64), :] = result[192:256]
+            result_ref[pl.ds(2 * FEAT, 64), :] = result[192:256]
         else:
-            value_out[mine, :] = result[192:288]
-            value_out[pl.ds(64, 32), :] = result[288:320]
+            result_ref[pl.ds(2 * FEAT + GF, GF), :] = result[192:288]
+            result_ref[pl.ds(2 * FEAT + 64, 32), :] = result[288:320]
 
     wait_all(wanted.at[pl.ds(1, OWNERS - 1)], send_sem.at[0])
     for g in range(GROUPS):
@@ -328,15 +346,20 @@
         wait_all(backs[g].at[pl.ds(SLOT, ROWS - SLOT)], send_sem.at[3 + g])
 
 
+def divide(result_ref, query_out, key_out, value_out):
+    for i, out in enumerate((query_out, key_out, value_out)):
+        out[...] = result_ref[pl.ds(i * FEAT, FEAT), :]
+
+
 def on_device(query, key_rows, value, out_grad, members):
     shape = jax.ShapeDtypeStruct(query.shape, BF16)
     vmem = pl.BlockSpec(memory_space=pltpu.VMEM)
-    return pl.pallas_call(
+    result = pl.pallas_call(
         kernel,
         name="hept_backward",
-        out_shape=(shape, shape, shape),
+        out_shape=jax.ShapeDtypeStruct((3 * FEAT, POINTS), BF16),
         in_specs=[pl.BlockSpec(memory_space=pl.ANY)] * 5,
-        out_specs=(vmem,) * 3,
+        out_specs=vmem,
         scratch_shapes=[
             *[pltpu.VMEM(query.shape, BF16)] * 4,
             pltpu.VMEM(members.shape, jnp.int32),
@@ -355,12 +378,15 @@
             *[pltpu.VMEM((ROWS, width), BF16) for width in BACK],
             pltpu.SemaphoreType.DMA((5,)),
             pltpu.SemaphoreType.DMA((5,)),
-            pltpu.SemaphoreType.DMA((CHUNKS + 4,)),
+            pltpu.SemaphoreType.DMA((CHUNKS + GROUPS + GROUPS * PARTS,)),
         ],
         compiler_params=pltpu.CompilerParams(
             collective_id=0, has_side_effects=True, vmem_limit_bytes=56 * 1024 * 1024
         ),
     )(query, key_rows, value, out_grad, members)
+    return pl.pallas_call(
+        divide, name="divide", out_shape=(shape,) * 3, in_specs=[vmem], out_specs=(vmem,) * 3
+    )(result)
 
 
 def solution(mesh):

time: 94.3 us -> 91.7 us (0.972); the launches traced: 92.9 us -> 91.5 us
  local copies, waits for them, and re-layouts: 3.33 us -> 0 us
  Pallas kernels: 88.9 us -> 90.9 us
    unnamed x7 -> x0, local copies, waits for them, and re-layouts: 3.33 us -> none
    pallas_call x1 -> x2, Pallas kernels: 88.9 us -> 90.9 us  [the longest x1 89 us: on_device(): pl.pallas_call(kernel, name='hept_backward', out_shape=jax.ShapeDtypeStru...]
where the time goes in v2:
time: 91.7 us; the launch traced here: 91.5 us
  Pallas kernels  90.9 us (99%)
    pallas_call x1, Pallas kernels, on_device(): pl.pallas_call(kernel, name='hept_backward', out_shape=jax.ShapeDtypeStru...  89 us
    pallas_call x1, Pallas kernels, on_device(): pl.pallas_call(divide, name='divide', out_shape=(shape,) * 3, in_specs=[v...  1.88 us

profile of v2, /device:TPU:1, one launch (start us, length us, event | category | flops | bytes accessed | tf_op | source)
XLA Modules:
  0.0 91.5 jit_solution(828710682946037654)
XLA Ops:
  0.6 89.0 %hept_backward.1.result_ref = bf16[576,512]{1,0:T(8,128)(2,1)} custom-call(bf16[192,512]{1,0:T(8,128)(2,1)} %query_any.1, bf16[192,512]{1,0:T(8,128)(2,1)} %key_any.1, bf16[192,512]{1,0:T(8,128)(2,1)} %value_any.1, bf16[192,512]{1,0:T(8,128)(2,1)} %grad_any.1, s32[3,4,128]{2,1,0:T(4,128)} %members_any.1), custom_call_target="tpu_custom_call" | custom-call | tf_op jit(solution)/shard_map/hept_backward/pallas_call | solution.py:357
  89.6 1.9 %divide.1 = (bf16[192,512]{1,0:T(8,128)(2,1)}, bf16[192,512]{1,0:T(8,128)(2,1)}, bf16[192,512]{1,0:T(8,128)(2,1)}) custom-call(bf16[576,512]{1,0:T(8,128)(2,1)} %hept_backward.1.result_ref), custom_call_target="tpu_custom_call" | custom-call | tf_op jit(solution)/shard_map/divide/pallas_call | solution.py:387

commit v3 on v2

--- a/solution.py
+++ b/solution.py
@@ -23,7 +23,9 @@
 GF = GH * HEAD_DIM
 WIDE = 4 * GF
 FEAT = HEADS * HEAD_DIM
-BACK = (256, 384)
+GRADS = (256, 384)
+BACK = 256
+TAIL = SLOT // 2
 CHUNK = 256
 CHUNKS = ROWS // CHUNK
 PER = CHUNK // SLOT
@@ -79,7 +81,7 @@
     result_ref,
     query_ref, key_ref, value_ref, grad_ref, members_ref,
     columns, wanted, requests, points0, points1, pick, pick_t, gather, gather_t,
-    out0, out1, in0, in1, rows_of, tiles, grads0, grads1, slots0, slots1, back0, back1, home0, home1,
+    out0, out1, in0, in1, rows_of, tiles, grads0, grads1, slots0, slots1, back0, back1, home0, home1, tail_back, tail_home,
     load_sem, send_sem, recv_sem,
 ):
     points_in, outs, ins = (points0, points1), (out0, out1), (in0, in1)
@@ -218,6 +220,12 @@
         iota((CHUNK, TABLES * TCHUNK), 0) == SLOT * (within // CAP) + CAP * (packed_lane // TCHUNK) + within % CAP
     )
 
+    tail_row = iota((PER * TAIL, TABLES * TCHUNK), 0)
+    within = iota((PER * TAIL, TABLES * TCHUNK), 1) % TCHUNK
+    source_row = SLOT * (within // CAP) + CAP * (iota((PER * TAIL, TABLES * TCHUNK), 1) // TCHUNK) + within % CAP
+    tail_row = SLOT * (tail_row // TAIL) + tail_row % TAIL
+    merge_tail = jnp.concatenate([onehot(tail_row == source_row), onehot(tail_row + TAIL == source_row)], axis=0)
+
     scale = HEAD_DIM**-0.5
     log2e = 1.4426950408889634
     feature = iota((BUCKET, GF), 1) // HEAD_DIM
@@ -295,13 +303,11 @@
         yield
         query_part = jnp.transpose(jnp.concatenate(paired(k_t, dscore_low), axis=0)).astype(BF16)
         key_part = (dot(dscore_low, spread_rows(q_low)) - sums * k_full).astype(BF16)
-        if g == 0:
-            grads0[span, :] = jnp.concatenate([query_part, key_part, value_part[:, :64]], axis=1)
-            grads1[span, 288:320] = value_part[:, 64:]
-        else:
-            grads1[span, 0:288] = jnp.concatenate([query_part, key_part, value_part], axis=1)
-
-    grads1[:, 256:384] = jnp.zeros((BUCKETS * BUCKET, 128), BF16)
+        grads[g][span, 0:256] = jnp.concatenate([query_part, key_part, value_part[:, :64]], axis=1)
+        at = 256 + 32 * (1 - g)
+        grads1[span, at : at + 32] = value_part[:, 64:]
+        grads1[span, at + 64 : at + 96] = value_part[:, 64:]
+
     for g in range(GROUPS):
         wait_all(ins[g].at[pl.ds(SLOT, ROWS - SLOT)], recv_sem.at[CHUNKS + g])
         for k in range(CHUNKS):
@@ -322,28 +328,51 @@
             slots[g][t] = dot(gather_t[t], grads[g][pl.ds(t * POINTS, POINTS), :]).astype(BF16)
         for k in range(CHUNKS):
             part = jnp.concatenate([slots[g][t, pl.ds(k * TCHUNK, TCHUNK), :] for t in range(TABLES)], axis=0)
-            backs[g][pl.ds(k * CHUNK, CHUNK), :] = dot(merge, part).astype(BF16)
-            send(backs[g], homes[g], k, -1, 3 + g, CHUNKS + GROUPS + g * PARTS + k // (CHUNKS // PARTS))
-
+            backs[g][pl.ds(k * CHUNK, CHUNK), :] = dot(merge, part[:, :BACK]).astype(BF16)
+            received = CHUNKS + GROUPS + k // (CHUNKS // PARTS)
+            send(backs[g], homes[g], k, -1, 3 + g, received + g * PARTS)
+            if g == 1:
+                both = dot(merge_tail, part[:, BACK:])
+                tail = jnp.where(iota((PER * TAIL, 128), 1) < 64, both[: PER * TAIL], both[PER * TAIL :])
+                tail_back[pl.ds(k * PER, PER)] = tail.reshape(PER, TAIL, 128).astype(BF16)
+                for step in range(max(1, k * PER), (k + 1) * PER):
+                    copy(tail_back.at[step], tail_home.at[step], step, -1, 5, received + 2 * PARTS).start()
+                if k == 0:
+                    tail_home[0] = tail_back[0]
+
+    part = ROWS // PARTS
+    tails = part // 2
+    wide = onehot(
+        iota((part, tails), 1) == TAIL * (iota((part, tails), 0) // SLOT) + iota((part, tails), 0) % TAIL
+    )
+    own_half = (iota((part, 128), 0) % SLOT < TAIL) == (iota((part, 128), 1) < 64)
     for g in range(GROUPS):
-        total = jnp.zeros((POINTS, BACK[g]), F32)
+        total = jnp.zeros((POINTS, GRADS[g]), F32)
         for p in range(PARTS):
-            part = ROWS // PARTS
-            wait_all(homes[g].at[pl.ds(max(SLOT, p * part), part - SLOT * (p == 0))], recv_sem.at[CHUNKS + GROUPS + g * PARTS + p])
-            total = total + dot(pick_t[:, p * part : (p + 1) * part], homes[g][pl.ds(p * part, part), :])
-        result = jnp.transpose(total).astype(BF16)
+            first = SLOT * (p == 0)
+            received = CHUNKS + GROUPS + p
+            wait_all(homes[g].at[pl.ds(p * part + first, part - first)], recv_sem.at[received + g * PARTS])
+            rows = homes[g][pl.ds(p * part, part), :]
+            if g == 1:
+                owners = part // SLOT
+                first = int(p == 0)
+                wait_all(tail_home.at[pl.ds(p * owners + first, owners - first)], recv_sem.at[received + 2 * PARTS])
+                tail = tail_home[pl.ds(p * owners, owners)].astype(F32).reshape(tails, 128).astype(BF16)
+                rows = jnp.concatenate([rows, jnp.where(own_half, dot(wide, tail), 0.0).astype(BF16)], axis=1)
+            total = total + dot(pick_t[:, p * part : (p + 1) * part], rows)
+        result = jnp.transpose(total)
         for i in range(2):
-            result_ref[pl.ds(i * FEAT + g * GF, GF), :] = result[i * GF : (i + 1) * GF]
-        if g == 0:
-            result_ref[pl.ds(2 * FEAT, 64), :] = result[192:256]
-        else:
-            result_ref[pl.ds(2 * FEAT + GF, GF), :] = result[192:288]
-            result_ref[pl.ds(2 * FEAT + 64, 32), :] = result[288:320]
+            result_ref[pl.ds(i * FEAT + g * GF, GF), :] = result[i * GF : (i + 1) * GF].astype(BF16)
+        result_ref[pl.ds(2 * FEAT + g * GF, 64), :] = result[192:256].astype(BF16)
+    last = (result[256:320] + result[320:384]).astype(BF16)
+    result_ref[pl.ds(2 * FEAT + GF + 64, 32), :] = last[:32]
+    result_ref[pl.ds(2 * FEAT + 64, 32), :] = last[32:]
 
     wait_all(wanted.at[pl.ds(1, OWNERS - 1)], send_sem.at[0])
     for g in range(GROUPS):
         wait_all(outs[g].at[pl.ds(SLOT, ROWS - SLOT)], send_sem.at[1 + g])
         wait_all(backs[g].at[pl.ds(SLOT, ROWS - SLOT)], send_sem.at[3 + g])
+    wait_all(tail_back.at[pl.ds(1, OWNERS - 1)], send_sem.at[5])
 
 
 def divide(result_ref, query_out, key_out, value_out):
@@ -372,13 +401,13 @@
             *[pltpu.VMEM((ROWS, WIDE), BF16)] * 4,
             pltpu.VMEM((TABLES, TROWS, WIDE), BF16),
             pltpu.VMEM((BUCKETS * BUCKET, WIDE), BF16),
-            *[pltpu.VMEM((BUCKETS * BUCKET, width), BF16) for width in BACK],
-            *[pltpu.VMEM((TABLES, TROWS, width), BF16) for width in BACK],
-            *[pltpu.VMEM((ROWS, width), BF16) for width in BACK],
-            *[pltpu.VMEM((ROWS, width), BF16) for width in BACK],
+            *[pltpu.VMEM((BUCKETS * BUCKET, width), BF16) for width in GRADS],
+            *[pltpu.VMEM((TABLES, TROWS, width), BF16) for width in GRADS],
+            *[pltpu.VMEM((ROWS, BACK), BF16)] * 4,
+            *[pltpu.VMEM((OWNERS, TAIL, 128), BF16)] * 2,
             pltpu.SemaphoreType.DMA((5,)),
-            pltpu.SemaphoreType.DMA((5,)),
-            pltpu.SemaphoreType.DMA((CHUNKS + GROUPS + GROUPS * PARTS,)),
+            pltpu.SemaphoreType.DMA((6,)),
+            pltpu.SemaphoreType.DMA((CHUNKS + GROUPS + 3 * PARTS,)),
         ],
         compiler_params=pltpu.CompilerParams(
             collective_id=0, has_side_effects=True, vmem_limit_bytes=56 * 1024 * 1024

time: 91.7 us -> 89.2 us (0.973)
  Pallas kernels: 90.9 us -> 88.4 us
    pallas_call x1, Pallas kernels: 89 us -> 86.5 us  [on_device(): pl.pallas_call(kernel, name='hept_backward', out_shape=jax.ShapeDtypeStru...]
where the time goes in v3:
time: 89.2 us; the launch traced here: 89 us
  Pallas kernels  88.4 us (99%)
    pallas_call x1, Pallas kernels, on_device(): pl.pallas_call(kernel, name='hept_backward', out_shape=jax.ShapeDtypeStru...  86.5 us
    pallas_call x1, Pallas kernels, on_device(): pl.pallas_call(divide, name='divide', out_shape=(shape,) * 3, in_specs=[v...  1.88 us

profile of v3, /device:TPU:1, one launch (start us, length us, event | category | flops | bytes accessed | tf_op | source)
XLA Modules:
  0.0 89.0 jit_solution(17896636515859651335)
XLA Ops:
  0.6 86.5 %hept_backward.1.result_ref = bf16[576,512]{1,0:T(8,128)(2,1)} custom-call(bf16[192,512]{1,0:T(8,128)(2,1)} %query_any.1, bf16[192,512]{1,0:T(8,128)(2,1)} %key_any.1, bf16[192,512]{1,0:T(8,128)(2,1)} %value_any.1, bf16[192,512]{1,0:T(8,128)(2,1)} %grad_any.1, s32[3,4,128]{2,1,0:T(4,128)} %members_any.1), custom_call_target="tpu_custom_call" | custom-call | tf_op jit(solution)/shard_map/hept_backward/pallas_call | solution.py:386
  87.1 1.9 %divide.1 = (bf16[192,512]{1,0:T(8,128)(2,1)}, bf16[192,512]{1,0:T(8,128)(2,1)}, bf16[192,512]{1,0:T(8,128)(2,1)}) custom-call(bf16[576,512]{1,0:T(8,128)(2,1)} %hept_backward.1.result_ref), custom_call_target="tpu_custom_call" | custom-call | tf_op jit(solution)/shard_map/divide/pallas_call | solution.py:416

commit v4 on v3

--- a/solution.py
+++ b/solution.py
@@ -30,7 +30,7 @@
 CHUNKS = ROWS // CHUNK
 PER = CHUNK // SLOT
 TCHUNK = PER * CAP
-TOGETHER = 2
+TOGETHER = 4
 PARTS = 4
 
 
@@ -252,9 +252,6 @@
                 blocks.append(jnp.concatenate(pieces, axis=0))
             return jnp.concatenate(blocks, axis=1).astype(BF16)
 
-        def spread_rows(part):
-            return jnp.concatenate([part * head for head in heads], axis=0)
-
         norms = jnp.concatenate(
             [
                 -0.5 * jnp.sum(k_t[h * HEAD_DIM : (h + 1) * HEAD_DIM] ** 2, axis=0, keepdims=True)
@@ -268,41 +265,51 @@
             terms.append(norms.astype(BF16).astype(F32))
             norms = norms - terms[-1]
         terms = jnp.transpose(jnp.concatenate(terms, axis=0)).astype(BF16)
-        logits = dot(jnp.concatenate([k_low, terms], axis=1), jnp.concatenate([spread_t(q_t), term_heads], axis=0))
-        dprob = dot(v_low, spread_t(g_t))
+        keys = jnp.concatenate([k_low, terms], axis=1)
+        queries = jnp.concatenate([spread_t(q_t), term_heads], axis=0)
+        cotangents = spread_t(g_t)
+        v_t_low, k_t_low = v_t.astype(BF16), k_t.astype(BF16)
+        sums = jnp.zeros((BUCKET, GF), F32)
+        key_sum, value_sum, query_rows = 0.0, 0.0, []
         yield
-        top = jnp.max(logits, axis=0, keepdims=True)
-        expons = jnp.exp2((logits - top) * (scale * log2e))
-        probs = expons * (1.0 / jnp.sum(expons, axis=0, keepdims=True))
-        probs_low = probs.astype(BF16)
-        yield
-
-        def paired(left, right):
-            left = left.astype(BF16)
-            parts = []
-            for u in range(GH // 2):
-                both = dot(left[2 * HEAD_DIM * u : 2 * HEAD_DIM * (u + 1)], right[:, 2 * BUCKET * u : 2 * BUCKET * (u + 1)])
-                parts += [both[:HEAD_DIM, :BUCKET], both[HEAD_DIM:, BUCKET:]]
-            return parts
-
-        delta = jnp.concatenate(
-            [
-                jnp.sum(part * g_t[h * HEAD_DIM : (h + 1) * HEAD_DIM], axis=0, keepdims=True)
-                for h, part in enumerate(paired(v_t, probs_low))
-            ],
-            axis=1,
-        )
-        value_part = dot(probs_low, spread_rows(g_low)).astype(BF16)
-        yield
-        dscore = scale * probs * (dprob - delta)
-        dscore_low = dscore.astype(BF16)
-        sums = jnp.zeros((BUCKET, GF), F32)
-        for h in range(GH):
-            total = jnp.sum(dscore[:, h * BUCKET : (h + 1) * BUCKET], axis=1, keepdims=True)
-            sums = jnp.where(feature == h, total, sums)
-        yield
-        query_part = jnp.transpose(jnp.concatenate(paired(k_t, dscore_low), axis=0)).astype(BF16)
-        key_part = (dot(dscore_low, spread_rows(q_low)) - sums * k_full).astype(BF16)
+        for u in range(GH // 2):
+            wide = slice(2 * BUCKET * u, 2 * BUCKET * (u + 1))
+            narrow = slice(2 * HEAD_DIM * u, 2 * HEAD_DIM * (u + 1))
+            logits = dot(keys, queries[:, wide])
+            dprob = dot(v_low, cotangents[:, wide])
+            yield
+            top = jnp.max(logits, axis=0, keepdims=True)
+            expons = jnp.exp2((logits - top) * (scale * log2e))
+            probs = expons * (1.0 / jnp.sum(expons, axis=0, keepdims=True))
+            probs_low = probs.astype(BF16)
+            yield
+            both = dot(v_t_low[narrow], probs_low)
+            outputs = (both[:HEAD_DIM, :BUCKET], both[HEAD_DIM:, BUCKET:])
+            delta = jnp.concatenate(
+                [
+                    jnp.sum(part * g_t[(2 * u + i) * HEAD_DIM : (2 * u + i + 1) * HEAD_DIM], axis=0, keepdims=True)
+                    for i, part in enumerate(outputs)
+                ],
+                axis=1,
+            )
+            value_sum = value_sum + dot(
+                probs_low, jnp.concatenate([g_low * heads[2 * u], g_low * heads[2 * u + 1]], axis=0)
+            )
+            yield
+            dscore = scale * probs * (dprob - delta)
+            dscore_low = dscore.astype(BF16)
+            for i in range(2):
+                total = jnp.sum(dscore[:, i * BUCKET : (i + 1) * BUCKET], axis=1, keepdims=True)
+                sums = jnp.where(feature == 2 * u + i, total, sums)
+            yield
+            both = dot(k_t_low[narrow], dscore_low)
+            query_rows += [both[:HEAD_DIM, :BUCKET], both[HEAD_DIM:, BUCKET:]]
+            key_sum = key_sum + dot(
+                dscore_low, jnp.concatenate([q_low * heads[2 * u], q_low * heads[2 * u + 1]], axis=0)
+            )
+        query_part = jnp.transpose(jnp.concatenate(query_rows, axis=0)).astype(BF16)
+        key_part = (key_sum - sums * k_full).astype(BF16)
+        value_part = value_sum.astype(BF16)
         grads[g][span, 0:256] = jnp.concatenate([query_part, key_part, value_part[:, :64]], axis=1)
         at = 256 + 32 * (1 - g)
         grads1[span, at : at + 32] = value_part[:, 64:]

time: 89.2 us -> 88.1 us (0.988)
  Pallas kernels: 88.4 us -> 87.3 us
    pallas_call x1, Pallas kernels: 86.5 us -> 85.4 us  [on_device(): pl.pallas_call(kernel, name='hept_backward', out_shape=jax.ShapeDtypeStru...]
where the time goes in v4:
time: 88.1 us; the launch traced here: 88 us
  Pallas kernels  87.3 us (99%)
    pallas_call x1, Pallas kernels, on_device(): pl.pallas_call(kernel, name='hept_backward', out_shape=jax.ShapeDtypeStru...  85.4 us
    pallas_call x1, Pallas kernels, on_device(): pl.pallas_call(divide, name='divide', out_shape=(shape,) * 3, in_specs=[v...  1.88 us

profile of v4, /device:TPU:1, one launch (start us, length us, event | category | flops | bytes accessed | tf_op | source)
XLA Modules:
  0.0 88.0 jit_solution(14841251588890670826)
XLA Ops:
  0.6 85.4 %hept_backward.1.result_ref = bf16[576,512]{1,0:T(8,128)(2,1)} custom-call(bf16[192,512]{1,0:T(8,128)(2,1)} %query_any.1, bf16[192,512]{1,0:T(8,128)(2,1)} %key_any.1, bf16[192,512]{1,0:T(8,128)(2,1)} %value_any.1, bf16[192,512]{1,0:T(8,128)(2,1)} %grad_any.1, s32[3,4,128]{2,1,0:T(4,128)} %members_any.1), custom_call_target="tpu_custom_call" | custom-call | tf_op jit(solution)/shard_map/hept_backward/pallas_call | solution.py:393
  86.1 1.9 %divide.1 = (bf16[192,512]{1,0:T(8,128)(2,1)}, bf16[192,512]{1,0:T(8,128)(2,1)}, bf16[192,512]{1,0:T(8,128)(2,1)}) custom-call(bf16[576,512]{1,0:T(8,128)(2,1)} %hept_backward.1.result_ref), custom_call_target="tpu_custom_call" | custom-call | tf_op jit(solution)/shard_map/divide/pallas_call | solution.py:423

commit v5 on v4

--- a/solution.py
+++ b/solution.py
@@ -110,10 +110,11 @@
             ]
         )
     ]
-    for load in loads:
-        load.start()
+    loads[0].start()
     for step in range(1, OWNERS):
         pl.semaphore_signal(barrier, inc=1, device_id=peer(step, 1), device_id_type=MESH)
+    for load in loads[1:]:
+        load.start()
     loads[0].wait()
 
     x, core, z, y = place()
@@ -190,12 +191,12 @@
         picked = onehot(dot(asks.astype(BF16), ones) == number)
         pick[rows, :] = picked
         out0[rows, :] = dot(picked, points0[...]).astype(BF16)
-        send(out0, in0, k, 1, 1, CHUNKS)
+        send(out0, in0, k, 1, 1, CHUNKS + k)
     turn_points(1)
     for k in range(CHUNKS):
         rows = pl.ds(k * CHUNK, CHUNK)
         out1[rows, :] = dot(pick[rows, :], points1[...]).astype(BF16)
-        send(out1, in1, k, 1, 2, CHUNKS + 1)
+        send(out1, in1, k, 1, 2, 2 * CHUNKS + k)
 
     @pl.loop(0, CHUNKS)
     def _(k):
@@ -316,8 +317,9 @@
         grads1[span, at + 64 : at + 96] = value_part[:, 64:]
 
     for g in range(GROUPS):
-        wait_all(ins[g].at[pl.ds(SLOT, ROWS - SLOT)], recv_sem.at[CHUNKS + g])
         for k in range(CHUNKS):
+            first = SLOT * (k == 0)
+            wait_all(ins[g].at[pl.ds(k * CHUNK + first, CHUNK - first)], recv_sem.at[(1 + g) * CHUNKS + k])
             part = dot(split, ins[g][pl.ds(k * CHUNK, CHUNK), :]).astype(BF16)
             for t in range(TABLES):
                 rows_of[t, pl.ds(k * TCHUNK, TCHUNK), :] = part[t * TCHUNK : (t + 1) * TCHUNK]
@@ -336,7 +338,7 @@
         for k in range(CHUNKS):
             part = jnp.concatenate([slots[g][t, pl.ds(k * TCHUNK, TCHUNK), :] for t in range(TABLES)], axis=0)
             backs[g][pl.ds(k * CHUNK, CHUNK), :] = dot(merge, part[:, :BACK]).astype(BF16)
-            received = CHUNKS + GROUPS + k // (CHUNKS // PARTS)
+            received = 3 * CHUNKS + k // (CHUNKS // PARTS)
             send(backs[g], homes[g], k, -1, 3 + g, received + g * PARTS)
             if g == 1:
                 both = dot(merge_tail, part[:, BACK:])
@@ -357,7 +359,7 @@
         total = jnp.zeros((POINTS, GRADS[g]), F32)
         for p in range(PARTS):
             first = SLOT * (p == 0)
-            received = CHUNKS + GROUPS + p
+            received = 3 * CHUNKS + p
             wait_all(homes[g].at[pl.ds(p * part + first, part - first)], recv_sem.at[received + g * PARTS])
             rows = homes[g][pl.ds(p * part, part), :]
             if g == 1:
@@ -414,7 +416,7 @@
             *[pltpu.VMEM((OWNERS, TAIL, 128), BF16)] * 2,
             pltpu.SemaphoreType.DMA((5,)),
             pltpu.SemaphoreType.DMA((6,)),
-            pltpu.SemaphoreType.DMA((CHUNKS + GROUPS + 3 * PARTS,)),
+            pltpu.SemaphoreType.DMA((3 * CHUNKS + 3 * PARTS,)),
         ],
         compiler_params=pltpu.CompilerParams(
             collective_id=0, has_side_effects=True, vmem_limit_bytes=56 * 1024 * 1024

time: 88.1 us -> 87.9 us (level)
  no operation moved by 1% of the time
where the time goes in v5:
time: 87.9 us; the launch traced here: 87.7 us
  Pallas kernels  87.1 us (99%)
    pallas_call x1, Pallas kernels, on_device(): pl.pallas_call(kernel, name='hept_backward', out_shape=jax.ShapeDtypeStru...  85.2 us
    pallas_call x1, Pallas kernels, on_device(): pl.pallas_call(divide, name='divide', out_shape=(shape,) * 3, in_specs=[v...  1.88 us

profile of v5, /device:TPU:1, one launch (start us, length us, event | category | flops | bytes accessed | tf_op | source)
XLA Modules:
  0.0 87.7 jit_solution(5558791298215990749)
XLA Ops:
  0.6 85.2 %hept_backward.1.result_ref = bf16[576,512]{1,0:T(8,128)(2,1)} custom-call(bf16[192,512]{1,0:T(8,128)(2,1)} %query_any.1, bf16[192,512]{1,0:T(8,128)(2,1)} %key_any.1, bf16[192,512]{1,0:T(8,128)(2,1)} %value_any.1, bf16[192,512]{1,0:T(8,128)(2,1)} %grad_any.1, s32[3,4,128]{2,1,0:T(4,128)} %members_any.1), custom_call_target="tpu_custom_call" | custom-call | tf_op jit(solution)/shard_map/hept_backward/pallas_call | solution.py:395
  85.8 1.9 %divide.1 = (bf16[192,512]{1,0:T(8,128)(2,1)}, bf16[192,512]{1,0:T(8,128)(2,1)}, bf16[192,512]{1,0:T(8,128)(2,1)}) custom-call(bf16[576,512]{1,0:T(8,128)(2,1)} %hept_backward.1.result_ref), custom_call_target="tpu_custom_call" | custom-call | tf_op jit(solution)/shard_map/divide/pallas_call | solution.py:425
